TPU v7x, 256 devices: a whole 4x4x8 slice. The times are simulated.
256 devices in a mesh: ens: 4 (over y), horiz: 64 (over x, z, core).
Axes of the slice: x: 4, y: 4, z: 8, core: 2. Of those that a mesh axis runs over, the one named last changes fastest.
Arguments:
- prognostic: float32 [4, 128, 256, 128], P('ens', None, 'horiz'), may hold values from -6 to 6
- diffusivity: float32 [4, 32, 256, 128], P('ens', None, 'horiz'), may hold values from 0.1 to 10
- mixing: float32 [2, 256, 128], P(None, 'horiz'), may hold values from 0.03 to 0.24
- cotangent: float32 [4, 128, 256, 128], P('ens', None, 'horiz'), may hold values from -6 to 6
- tile_cols: int32 [4, 64, 3, 128], P('ens', 'horiz'), may hold values from 0 to 511, as said below
- pad_mask: int32 [4, 64, 3, 128], P('ens', 'horiz'), may hold values 0 or 1
- tile_count: int32 [4, 64], P('ens', 'horiz'), may hold values from 1 to 3, as said below
- w_in: bfloat16 [1024, 128], replicated, may hold values from -0.5 to 0.5
- w_mid: bfloat16 [1024, 1024], replicated, may hold values from -0.1875 to 0.1875
- w_out: bfloat16 [128, 1024], replicated, may hold values from -0.1875 to 0.1875
Outputs:
- state_next: float32 [4, 128, 256, 128], P('ens', None, 'horiz')
- state_grad: float32 [4, 128, 256, 128], P('ens', None, 'horiz')
- grad_in: float32 [1024, 128], replicated
- grad_mid: float32 [1024, 1024], replicated
- grad_out: float32 [128, 1024], replicated
Inputs may be any that keep to these rules, and one draw needn't show every extreme that they name: `tile_cols`: within one member and block all 3 x 128 entries name different columns. Tiles 0 to tile_count - 1 of a block are in use; in every member some block uses all 3.
All inputs are finite; a program needn't handle non-finite values. No bound on the sum of `pad_mask` on one device may be relied on, other than what follows from the above.
Results may differ from a plain program's by a relative error of at most 0.0071.
Values may be sent and summed in bfloat16 or wider, within the bound.
A program may use at most 64 MiB of HBM per device.

v0:
```python
import math

import jax
import jax.numpy as jnp
from jax import lax
from jax.sharding import PartitionSpec as P

DYN_STEPS = 2


def shifted(block, axis, distance):
    devices = range(lax.axis_size(axis))
    route = [((i - distance) % len(devices), i) for i in devices]
    return lax.ppermute(block, axis, route)


def with_halo(block, sides, width):
    for axis, dim in sides:
        count = lax.axis_size(axis)
        forward = [(i, i + 1) for i in range(count - 1)]
        forward.append((count - 1, 0))
        backward = [(target, source) for source, target in forward]
        low = lax.ppermute(
            lax.slice_in_dim(block, block.shape[dim] - width, None, axis=dim), axis, forward
        )
        high = lax.ppermute(lax.slice_in_dim(block, 0, width, axis=dim), axis, backward)
        block = jnp.concatenate([low, block, high], axis=dim)
    return block


def silu_slope(pre_act):
    sigma_val = jax.nn.sigmoid(pre_act)
    return sigma_val * (1.0 + pre_act * (1.0 - sigma_val))


def vertical_solve(coefficient, right_side):
    coef_below = jnp.concatenate([jnp.zeros_like(coefficient[:1]), coefficient[:-1]], axis=0)
    coef_above = jnp.concatenate([coefficient[:-1], jnp.zeros_like(coefficient[:1])], axis=0)
    diag_term = 1.0 + coef_below + coefficient
    by_level = jnp.transpose(right_side, (1, 0, 2))

    def sweep_down(carried, inputs):
        prev_ratio, prev_value = carried
        below_now, above_now, diag_now, right_now = inputs
        divisor = diag_now + below_now * prev_ratio
        ratio_now = -above_now / divisor
        value_now = (right_now + below_now * prev_value) / divisor
        return ((ratio_now, value_now), (ratio_now, value_now))

    start_state = (jnp.zeros_like(coefficient[0]), jnp.zeros_like(by_level[0]))
    _, (ratios, values) = lax.scan(
        sweep_down, start_state, (coef_below, coef_above, diag_term, by_level)
    )

    def sweep_up(carried, inputs):
        ratio_now, value_now = inputs
        result = value_now - ratio_now * carried
        return (result, result)

    _, solved = lax.scan(sweep_up, jnp.zeros_like(by_level[0]), (ratios, values), reverse=True)
    return jnp.transpose(solved, (1, 0, 2))


def column_physics(x_tile, coef_tile, cot_tile, w_in, w_mid, w_out):
    fields = x_tile.shape[0]
    levels = coef_tile.shape[0]
    var_count = fields // levels
    contract_cols = (((1,), (1,)), ((), ()))
    contract_rows = (((0,), (0,)), ((), ()))
    pre_one = jnp.dot(w_in, x_tile, preferred_element_type=jnp.float32)
    act_one = jax.nn.silu(pre_one).astype(jnp.bfloat16)
    pre_two = jnp.dot(w_mid, act_one, preferred_element_type=jnp.float32)
    act_two = jax.nn.silu(pre_two).astype(jnp.bfloat16)
    tendency = jnp.dot(w_out, act_two, preferred_element_type=jnp.float32)
    coefficient = coef_tile.astype(jnp.float32)
    forced = (x_tile.astype(jnp.float32) + tendency).reshape(var_count, levels, -1)
    new_tile = vertical_solve(coefficient, forced).reshape(fields, -1)
    adjoint = vertical_solve(
        coefficient, cot_tile.astype(jnp.float32).reshape(var_count, levels, -1)
    ).reshape(fields, -1)
    adjoint_half = adjoint.astype(jnp.bfloat16)
    grad_out = lax.dot_general(
        adjoint_half, act_two, contract_cols, preferred_element_type=jnp.float32
    )
    back_two = lax.dot_general(
        w_out, adjoint_half, contract_rows, preferred_element_type=jnp.float32
    )
    delta_two = (back_two * silu_slope(pre_two)).astype(jnp.bfloat16)
    grad_mid = lax.dot_general(
        delta_two, act_one, contract_cols, preferred_element_type=jnp.float32
    )
    back_one = lax.dot_general(w_mid, delta_two, contract_rows, preferred_element_type=jnp.float32)
    delta_one = (back_one * silu_slope(pre_one)).astype(jnp.bfloat16)
    grad_in = lax.dot_general(delta_one, x_tile, contract_cols, preferred_element_type=jnp.float32)
    grad_x = adjoint + lax.dot_general(
        w_in, delta_one, contract_rows, preferred_element_type=jnp.float32
    )
    return (new_tile.astype(jnp.bfloat16), grad_x.astype(jnp.bfloat16), grad_in, grad_mid, grad_out)


def lat_flux(field_now, coef_lat):
    rising = jnp.concatenate(
        [field_now[..., 1:] - field_now[..., :-1], jnp.zeros_like(field_now[..., :1])], axis=-1
    )
    north_flux = coef_lat * rising
    south_flux = jnp.concatenate(
        [jnp.zeros_like(north_flux[..., :1]), north_flux[..., :-1]], axis=-1
    )
    return north_flux - south_flux


def padded_step(padded, lon_coef, lat_coef):
    inner_cells = padded[..., 1:-1, :]
    east_flux = lon_coef[1:-1] * (padded[..., 2:, :] - inner_cells)
    west_flux = lon_coef[:-2] * (inner_cells - padded[..., :-2, :])
    return inner_cells + east_flux - west_flux + lat_flux(inner_cells, lat_coef[1:-1])


def run_tiles(x_all, coef_all, cot_all, live_count, visit_order, w_in, w_mid, w_out):
    start_state = (
        jnp.zeros(x_all.shape, jnp.bfloat16),
        jnp.zeros(x_all.shape, jnp.bfloat16),
        jnp.zeros(w_in.shape, jnp.float32),
        jnp.zeros(w_mid.shape, jnp.float32),
        jnp.zeros(w_out.shape, jnp.float32),
    )

    def visit_tile(position, carried):
        state_acc, grad_acc, sum_in, sum_mid, sum_out = carried
        slot_now = visit_order[position]
        x_tile = lax.dynamic_index_in_dim(x_all, slot_now, 0, keepdims=False)
        coef_tile = lax.dynamic_index_in_dim(coef_all, slot_now, 0, keepdims=False)
        cot_tile = lax.dynamic_index_in_dim(cot_all, slot_now, 0, keepdims=False)
        new_tile, grad_x, grad_in, grad_mid, grad_out = column_physics(
            x_tile, coef_tile, cot_tile, w_in, w_mid, w_out
        )
        state_acc = lax.dynamic_update_index_in_dim(state_acc, new_tile, slot_now, 0)
        grad_acc = lax.dynamic_update_index_in_dim(grad_acc, grad_x, slot_now, 0)
        return (state_acc, grad_acc, sum_in + grad_in, sum_mid + grad_mid, sum_out + grad_out)

    finished = lax.fori_loop(0, live_count, visit_tile, start_state)
    return (finished[0], finished[1], (finished[2], finished[3], finished[4]))


def per_device(
    prognostic, diffusivity, mixing, cotangent, tile_cols, pad_mask, tile_count, w_in, w_mid, w_out
):
    fields = prognostic.shape[1]
    lon_local = prognostic.shape[2]
    latitudes = prognostic.shape[3]
    cells = lon_local * latitudes
    levels = diffusivity.shape[1]
    edge_coef = shifted(mixing[0, -1:, :], "horiz", 1)
    blank_row = jnp.zeros_like(edge_coef)
    lon_pad = jnp.concatenate([edge_coef, mixing[0], blank_row], axis=0)
    lat_pad = jnp.concatenate([blank_row, mixing[1], blank_row], axis=0)

    def advance(field_now):
        for repeat in range(DYN_STEPS):
            padded = with_halo(field_now, (("horiz", 2),), 1)
            field_now = padded_step(padded, lon_pad, lat_pad)
        return field_now

    moved = advance(prognostic)
    columns = tile_cols[0, 0].reshape(-1)
    tiles = tile_cols.shape[2]
    tile_width = tile_cols.shape[3]

    def to_tiles(field_flat):
        row_count = field_flat.shape[0]
        return jnp.transpose(
            field_flat[:, columns].reshape(row_count, tiles, tile_width), (1, 0, 2)
        )

    tile_total = tile_count[0, 0]
    active = (jnp.arange(tiles, dtype=jnp.int32) < tile_total).astype(jnp.int32)
    live_mask = pad_mask[0, 0] * active[:, None]
    moved_flat = moved[0].reshape(fields, cells)
    cot_flat = cotangent[0].reshape(fields, cells)
    x_tiles = to_tiles(moved_flat).astype(jnp.bfloat16)
    coef_tiles = to_tiles(diffusivity[0].reshape(levels, cells)).astype(jnp.bfloat16)
    cot_tiles = (to_tiles(cot_flat) * live_mask[:, None, :].astype(jnp.float32)).astype(
        jnp.bfloat16
    )
    state_tiles, grad_tiles, grad_sums = run_tiles(
        x_tiles,
        coef_tiles,
        cot_tiles,
        tile_total,
        jnp.arange(tiles, dtype=jnp.int32),
        w_in,
        w_mid,
        w_out,
    )
    live_flat = live_mask.reshape(-1)

    def place_back(field_flat, tile_vals):
        fresh_vals = jnp.transpose(tile_vals, (1, 0, 2)).reshape(fields, -1).astype(jnp.float32)
        kept_vals = field_flat[:, columns]
        return field_flat.at[:, columns].set(
            jnp.where(live_flat[None, :] > 0, fresh_vals, kept_vals)
        )

    state_next = place_back(moved_flat, state_tiles).reshape(prognostic.shape)
    grad_field = place_back(cot_flat, grad_tiles).reshape(prognostic.shape)
    state_grad = advance(grad_field)
    summed = lax.psum((grad_sums[0], grad_sums[1], grad_sums[2]), ("ens", "horiz"))
    column_total = lax.axis_size("ens") * lax.axis_size("horiz") * cells
    factor = 1.0 / math.sqrt(column_total)
    return (state_next, state_grad, summed[0] * factor, summed[1] * factor, summed[2] * factor)


def solution(mesh):
    placed = (
        P("ens", None, "horiz", None),
        P("ens", None, "horiz", None),
        P(None, "horiz", None),
        P("ens", None, "horiz", None),
        P("ens", "horiz", None, None),
        P("ens", "horiz", None, None),
        P("ens", "horiz"),
        P(),
        P(),
        P(),
    )
    return jax.shard_map(
        per_device,
        mesh=mesh,
        in_specs=placed,
        out_specs=(P("ens", None, "horiz", None), P("ens", None, "horiz", None), P(), P(), P()),
        check_vma=False,
    )
```

profile of v0, /device:TPU:1, one launch (start us, length us, event | category | flops | bytes accessed | tf_op | source)
XLA Modules:
  0.0 404.8 jit_solution(7823194989502532603)
XLA Ops:
  8.0 3.0 collective-permute-start.1
  11.0 1.2 fusion.78
  12.5 1.5 collective-permute-start.2
  14.7 1.3 slice_subtract_fusion.3
  17.3 1.1 copy.45
  18.4 1.1 gather_fusion.2
  20.7 1.4 gather_fusion
  23.0 4.3 %collective-permute-start.3 = (f32[1,128,1,128]{3,2,1,0:T(1,128)S(1)}, f32[1,128,1,128]{3,2,1,0:T(1,128)S(1)}, u32[]{:S(2)}, u32[]{:S(2)}) collective-permute-start(f32[1,128,1,128]{3,2,1,0:T(1,128)S(1)} %get-tuple-element.911), channel_id=1, source_target_pairs={{1,0},{2,1},{3,2},{4,3},{5,4},{6,5},{7,6},{8,7},{9,8},{10,9},{11,1... | collective-permute-start | bytes 196616 | tf_op jit(solution)/shard_map/ppermute | solution.py:26
  28.2 4.9 %collective-permute-done.4 = f32[1,128,1,128]{3,2,1,0:T(1,128)S(1)} collective-permute-done((f32[1,128,1,128]{3,2,1,0:T(1,128)S(1)}, f32[1,128,1,128]{3,2,1,0:T(1,128)S(1)}, u32[]{:S(2)}, u32[]{:S(2)}) %collective-permute-start.4) | collective-permute-done | bytes 65568 | tf_op jit(solution)/shard_map/ppermute | solution.py:23
  33.7 1.1 gather_fusion.1
  35.2 2.5 broadcast_in_dim.81
  37.7 28.6 %while.153 = (s32[]{:T(128)}, bf16[3,128,128]{2,1,0:T(8,128)(2,1)S(1)}, bf16[3,128,128]{1,2,0:T(8,128)(2,1)S(1)}, f32[1024,128]{1,0:T(8,128)S(1)}, f32[1024,1024...) while((s32[]{:T(128)}, ...), condition=%wide.region_9.10_spmd, body=%wide.region_0.9_spmd.sunk | while | flops 1013084416 | bytes 67982240 | solution.py:141
  41.4 2.4 convolution_bitcast_fusion.9
  44.6 3.8 while.154
  48.4 2.0 while.155
  50.4 4.5 %while.156 = (s32[]{:T(128)}, f32[128]{0:T(128)S(1)}, f32[4,128]{1,0:T(4,128)S(1)}, f32[32,128]{1,0:T(8,128)S(1)}, f32[32,4,128]{2,1,0:T(4,128)S(1)}, /*index=5*...) while((s32[]{:T(128)}, f32[128]{0:T(128)S(1)}, ...), condition=%wide.region_6.6_spmd.clone, body=%wide.region_5.5_spmd.clone.sunk | while | flops 2691 | bytes 18580 | solution.py:51
  54.9 3.0 while.157
  58.1 1.6 fusion.127
  59.7 1.5 convolution_add_fusion.8
  62.4 1.3 convolution_add_fusion.7
  63.6 2.0 copy-done.1
  67.7 1.8 scatter_custom_fusion.1
  69.7 6.3 %collective-permute-start.5 = (f32[1,128,1,128]{3,2,1,0:T(1,128)S(1)}, f32[1,128,1,128]{3,2,1,0:T(1,128)S(1)}, u32[]{:S(2)}, u32[]{:S(2)}) collective-permute-start(f32[1,128,1,128]{3,2,1,0:T(1,128)S(1)} %get-tuple-element.909), channel_id=1, source_target_pairs={{1,0},{2,1},{3,2},{4,3},{5,4},{6,5},{7,6},{8,7},{9,8},{10,9},{11,1... | collective-permute-start | bytes 196616 | tf_op jit(solution)/shard_map/ppermute | solution.py:26
  76.0 19.6 %collective-permute-start.6 = (f32[1,128,1,128]{3,2,1,0:T(1,128)S(1)}, f32[1,128,1,128]{3,2,1,0:T(1,128)S(1)}, u32[]{:S(2)}, u32[]{:S(2)}) collective-permute-start(f32[1,128,1,128]{3,2,1,0:T(1,128)S(1)} %get-tuple-element.910), channel_id=1, source_target_pairs={{0,1},{1,2},{2,3},{3,4},{4,5},{5,6},{6,7},{7,8},{8,9},{9,10},{10,1... | collective-permute-start | bytes 196616 | tf_op jit(solution)/shard_map/ppermute | solution.py:23
  95.9 1.6 scatter_custom_fusion
  99.0 1.7 collective-permute-start.8
  101.0 1.7 collective-permute-done.7
  102.7 1.1 fusion.38
  103.8 285.2 %all-reduce.12.cloned.1.call-done = (f32[1024,128]{1,0:T(8,128)}, f32[1024,1024]{1,0:T(8,128)}, f32[128,1024]{1,0:T(8,128)}) async-done(((f32[1024,128]{1,0:T(8,128)}, f32[1024,1024]{1,0:T(8,128)}, f32[128,1024]{1,0:T(8,128)}), (f32[1024,128]{1,0:T(8,128)}, f32[1024,1024]{1,0:T(8,128)}, f32[128,1024]{1,0:T(8,128)})) %all-reduce.12.cloned.1.call-update) | async-done | bytes 5242896 | tf_op jit(solution)/shard_map/psum | solution.py:207
  389.1 1.9 broadcast_multiply_fusion.2
  390.9 1.9 broadcast_multiply_fusion.1
  392.8 5.1 %broadcast_multiply_fusion = f32[1024,1024]{1,0:T(8,128)} fusion(f32[1024,1024]{1,0:T(8,128)} %get-tuple-element.890), kind=kLoop, calls=%fused_computation.83 | loop fusion | flops 1048576 | bytes 8388608 | tf_op jit(solution)/shard_map/mul | solution.py:210
  (549 shorter events, 22.0 us)
Async XLA Ops:
  7.2 15.1 %copy-start.4 = (f32[1,128,4,128]{3,2,1,0:T(4,128)S(1)}, f32[1,128,4,128]{3,2,1,0:T(4,128)}, u32[]{:S(2)}) copy-start(f32[1,128,4,128]{3,2,1,0:T(4,128)} %param.20) | copy-start | bytes 786436
  7.2 13.3 %copy-start.6 = (f32[1,32,4,128]{3,2,1,0:T(4,128)S(1)}, f32[1,32,4,128]{3,2,1,0:T(4,128)}, u32[]{:S(2)}) copy-start(f32[1,32,4,128]{3,2,1,0:T(4,128)} %param.21) | copy-start | bytes 196612
  7.2 381.9 %all-reduce.12.cloned.1.call-start = ((), (), s32[]{:S(2)}) async-start(), calls=%async_computation | async-start | bytes 10485760 | tf_op jit(solution)/shard_map/psum | solution.py:207
  8.0 14.2 %collective-permute-start.1 = (f32[1,128]{1,0:T(1,128)S(1)}, f32[1,128]{1,0:T(1,128)S(1)}, u32[]{:S(2)}, u32[]{:S(2)}) collective-permute-start(f32[1,128]{1,0:T(1,128)S(1)} %slice_bitcast_fusion.3), channel_id=1, source_target_pairs={{63,0},{0,1},{1,2},{2,3},{3,4},{4,5},{5,6},{6,7},{7,8},{8,9},{9,10... | collective-permute-start | bytes 1544 | tf_op jit(solution)/shard_map/ppermute | solution.py:14
  12.2 10.1 %collective-permute-start = (f32[1,128,1,128]{3,2,1,0:T(1,128)S(1)}, f32[1,128,1,128]{3,2,1,0:T(1,128)S(1)}, u32[]{:S(2)}, u32[]{:S(2)}) collective-permute-start(f32[1,128,1,128]{3,2,1,0:T(1,128)S(1)} %get-tuple-element.913), channel_id=1, source_target_pairs={{1,0},{2,1},{3,2},{4,3},{5,4},{6,5},{7,6},{8,7},{9,8},{10,9},{11,1... | collective-permute-start | bytes 196616 | tf_op jit(solution)/shard_map/ppermute | solution.py:26
  12.5 9.8 %collective-permute-start.2 = (f32[1,128,1,128]{3,2,1,0:T(1,128)S(1)}, f32[1,128,1,128]{3,2,1,0:T(1,128)S(1)}, u32[]{:S(2)}, u32[]{:S(2)}) collective-permute-start(f32[1,128,1,128]{3,2,1,0:T(1,128)S(1)} %get-tuple-element.914), channel_id=1, source_target_pairs={{0,1},{1,2},{2,3},{3,4},{4,5},{5,6},{6,7},{7,8},{8,9},{9,10},{10,1... | collective-permute-start | bytes 196616 | tf_op jit(solution)/shard_map/ppermute | solution.py:23
  23.0 5.2 %collective-permute-start.3 = (f32[1,128,1,128]{3,2,1,0:T(1,128)S(1)}, f32[1,128,1,128]{3,2,1,0:T(1,128)S(1)}, u32[]{:S(2)}, u32[]{:S(2)}) collective-permute-start(f32[1,128,1,128]{3,2,1,0:T(1,128)S(1)} %get-tuple-element.911), channel_id=1, source_target_pairs={{1,0},{2,1},{3,2},{4,3},{5,4},{6,5},{7,6},{8,7},{9,8},{10,9},{11,1... | collective-permute-start | bytes 196616 | tf_op jit(solution)/shard_map/ppermute | solution.py:26
  27.3 5.8 %collective-permute-start.4 = (f32[1,128,1,128]{3,2,1,0:T(1,128)S(1)}, f32[1,128,1,128]{3,2,1,0:T(1,128)S(1)}, u32[]{:S(2)}, u32[]{:S(2)}) collective-permute-start(f32[1,128,1,128]{3,2,1,0:T(1,128)S(1)} %get-tuple-element.912), channel_id=1, source_target_pairs={{0,1},{1,2},{2,3},{3,4},{4,5},{5,6},{6,7},{7,8},{8,9},{9,10},{10,1... | collective-permute-start | bytes 196616 | tf_op jit(solution)/shard_map/ppermute | solution.py:23
  33.6 4.1 %copy-start.2 = (bf16[1024,128]{1,0:T(8,128)(2,1)S(1)}, bf16[1024,128]{1,0:T(8,128)(2,1)}, u32[]{:S(2)}) copy-start(bf16[1024,128]{1,0:T(8,128)(2,1)} %param.27) | copy-start | bytes 786436
  33.6 4.1 %copy-start.7 = (pred[32]{0:T(512)(128)(4,1)S(1)}, pred[32]{0:T(512)(128)(4,1)}, u32[]{:S(2)}) copy-start(pred[32]{0:T(512)(128)(4,1)} %constant.183.clone.1) | copy-start | bytes 100
  41.0 2.8 copy-start.10
  43.8 0.8 copy-start.11
  58.1 3.1 copy-start.9
  59.7 2.7 copy-start
  63.6 2.0 copy-start.1
  66.3 0.8 copy-start.3
  66.3 1.0 copy-start.5
  66.3 1.0 copy-start.8
  69.7 28.7 %collective-permute-start.5 = (f32[1,128,1,128]{3,2,1,0:T(1,128)S(1)}, f32[1,128,1,128]{3,2,1,0:T(1,128)S(1)}, u32[]{:S(2)}, u32[]{:S(2)}) collective-permute-start(f32[1,128,1,128]{3,2,1,0:T(1,128)S(1)} %get-tuple-element.909), channel_id=1, source_target_pairs={{1,0},{2,1},{3,2},{4,3},{5,4},{6,5},{7,6},{8,7},{9,8},{10,9},{11,1... | collective-permute-start | bytes 196616 | tf_op jit(solution)/shard_map/ppermute | solution.py:26
  76.0 22.3 %collective-permute-start.6 = (f32[1,128,1,128]{3,2,1,0:T(1,128)S(1)}, f32[1,128,1,128]{3,2,1,0:T(1,128)S(1)}, u32[]{:S(2)}, u32[]{:S(2)}) collective-permute-start(f32[1,128,1,128]{3,2,1,0:T(1,128)S(1)} %get-tuple-element.910), channel_id=1, source_target_pairs={{0,1},{1,2},{2,3},{3,4},{4,5},{5,6},{6,7},{7,8},{8,9},{9,10},{10,1... | collective-permute-start | bytes 196616 | tf_op jit(solution)/shard_map/ppermute | solution.py:23
  98.9 3.8 collective-permute-start.7
  99.0 3.7 collective-permute-start.8
Sparse Core Ops, SparseCore 0:
  67.4 321.6 all-reduce.11
where the time goes:
time: 406 us; the launch traced here: 405 us
  waiting for transfers between devices  293 us (72%)
  starting transfers between devices  37 us (9%)
  local copies, waits for them, and re-layouts  25.1 us (6%)
  other arithmetic  19.1 us (5%)
  between operations  15.1 us (4%)
  matrix products  8.44 us (2%)
  loops' own time  7.49 us (2%)
    psum x1, waiting for transfers between devices, per_device(): lax.psum((grad_sums[0], grad_sums[1], grad_sums[2]), ('ens', 'horiz'))  285 us
    ppermute x4, starting transfers between devices, with_halo(): lax.ppermute(lax.slice_in_dim(block, block.shape[dim] - width, None, axis...  22.9 us
    ppermute x4, starting transfers between devices, with_halo(): lax.ppermute(lax.slice_in_dim(block, 0, width, axis=dim), axis, backward)  11 us
  transfers between devices with their start and end apart: 10, of which 4 were waited for; matrix products, arithmetic and copies ran while one was open for 4% of the time, Pallas kernels for 0%

commit v1 on v0

v1 whole, which is shorter than its diff:
```python
import functools
import math

import jax
import jax.numpy as jnp
from jax import lax
from jax.experimental import pallas as pl
from jax.experimental.pallas import tpu as pltpu
from jax.sharding import PartitionSpec as P

MESH = pl.DeviceIdType.MESH
LONS = 4
CHUNKS = 5
CHUNK_ROWS = 256
F32 = jnp.float32
BF16 = jnp.bfloat16
NT = (((1,), (1,)), ((), ()))
TN = (((0,), (0,)), ((), ()))


def sigmoid(value):
    return 0.5 * jnp.tanh(0.5 * value) + 0.5


def window_kernel(
    sizes,
    factor,
    prog_hbm,
    diff_hbm,
    mix_hbm,
    cot_hbm,
    cols_hbm,
    pad_hbm,
    count_hbm,
    win_hbm,
    wmid_hbm,
    wout_hbm,
    state_ref,
    sgrad_ref,
    full_ref,
    prog,
    diff,
    mix,
    cot,
    cols,
    pad,
    count,
    w_in,
    w_mid,
    w_out,
    halo_out,
    halo_in,
    mix_in,
    mid_step,
    moved,
    recip,
    ratio,
    adj,
    forced,
    gfield,
    x_half,
    adj_half,
    back_two,
    slope_one,
    act_one,
    act_two,
    delta_one,
    delta_two,
    part_f,
    part_b,
    got0,
    sum1_f,
    sum1_b,
    got1,
    sum2_f,
    sum2_b,
    got2,
    sum3_f,
    sum3_b,
    got3,
    owned,
    zfull,
    load_sem,
    halo_send,
    halo_recv,
    s0_send,
    s0_recv,
    s1_send,
    s1_recv,
    s2_send,
    s2_recv,
    s3_send,
    s3_recv,
    g3_send,
    g3_recv,
    g2_send,
    g2_recv,
    g1_send,
    g1_recv,
    g0_send,
    g0_recv,
):
    n, nz, levels, variables = sizes
    fields = levels * variables
    units = w_mid.shape[0]
    half = units // 2
    ring = n * nz * 2
    y = lax.axis_index("ens")
    h = lax.axis_index("horiz")
    core = h % 2
    z = (h // 2) % nz
    x = h // (2 * nz)
    right = (h + 1) % ring
    left = (h + ring - 1) % ring
    partner = h + 1 - 2 * core
    pieces = 2 * n
    rows = CHUNK_ROWS // pieces
    width = half // n
    zrows = owned.shape[0]

    def at_x(step):
        return (x + step) % n

    def at_y(step):
        return (y + step) % n

    def at_z(step):
        return (z + step) % nz

    def place(xi, zi, ci):
        return (xi * nz + zi) * 2 + ci

    barrier = pltpu.get_barrier_semaphore()
    greeted = [(at_y(s), h) for s in range(1, n)]
    greeted += [(y, place(at_x(s), z, core)) for s in range(1, n)]
    greeted += [(y, place(x, at_z(s), core)) for s in range(1, nz)]
    greeted += [(y, right), (y, left)]
    for peer in greeted:
        pl.semaphore_signal(barrier, inc=1, device_id=peer, device_id_type=MESH)

    loads = []
    for slot, (source, target) in enumerate(
        [
            (prog_hbm, prog),
            (mix_hbm, mix),
            (cols_hbm, cols),
            (pad_hbm, pad),
            (count_hbm, count),
            (diff_hbm, diff),
            (cot_hbm, cot),
            (wout_hbm, w_out),
            (win_hbm, w_in),
            (wmid_hbm, w_mid),
        ]
    ):
        copy = pltpu.make_async_copy(source, target, load_sem.at[slot])
        copy.start()
        loads.append(copy)

    sent = []

    def send(src, dst, send_sem, recv_sem, peer):
        copy = pltpu.make_async_remote_copy(
            src_ref=src,
            dst_ref=dst,
            send_sem=send_sem,
            recv_sem=recv_sem,
            device_id=peer,
            device_id_type=MESH,
        )
        copy.start()
        sent.append(copy)
        return copy

    def lon_rows(lon):
        return pl.ds(lon, fields, stride=LONS)

    def lon_cols(lon):
        return pl.ds(lon * 128, 128)

    def send_halo(which):
        return [
            send(
                halo_out.at[which, 0],
                halo_in.at[which, 0],
                halo_send.at[which, 0],
                halo_recv.at[which, 0],
                (y, right),
            ),
            send(
                halo_out.at[which, 1],
                halo_in.at[which, 1],
                halo_send.at[which, 1],
                halo_recv.at[which, 1],
                (y, left),
            ),
        ]

    loads[0].wait()
    for lon in range(LONS):
        halo_out[0, 1 - lon // 2, lon % 2] = prog[lon_rows(lon), :].astype(BF16)
    loads[1].wait()
    pl.semaphore_wait(barrier, len(greeted))
    halo_one = send_halo(0)
    mix_copies = [
        send(mix, mix_in.at[0], halo_send.at[2, 0], halo_recv.at[2, 0], (y, right)),
        send(mix, mix_in.at[1], halo_send.at[2, 1], halo_recv.at[2, 1], (y, left)),
    ]

    for copy in loads[2:7]:
        copy.wait()
    lon_of = lax.broadcasted_iota(jnp.int32, (16, 128), 0)
    lat_of = lax.broadcasted_iota(jnp.int32, (128, 128), 0)
    used = count[0, 0]
    live = jnp.zeros((16, 128), F32)
    for tile in range(cols.shape[0]):
        column = cols[tile]
        flag = jnp.where(tile < used, pad[tile], 0)
        lon_hit = (lon_of == column // 128) & (jnp.broadcast_to(flag, (16, 128)) > 0)
        lat_hit = lat_of == column % 128
        live = live + lax.dot_general(
            jnp.where(lon_hit, 1.0, 0.0).astype(BF16),
            jnp.where(lat_hit, 1.0, 0.0).astype(BF16),
            NT,
            preferred_element_type=F32,
        )
    live4 = live[:LONS]

    def level_rows(var, level):
        return pl.ds((var * levels + level) * LONS, LONS)

    def coefficient(level):
        return diff[level * LONS : (level + 1) * LONS, :].astype(BF16).astype(F32)

    below = jnp.zeros((LONS, 128), F32)
    last_ratio = jnp.zeros((LONS, 128), F32)
    for level in range(levels):
        here = coefficient(level)
        inverse = 1.0 / (1.0 + below + here + below * last_ratio)
        last_ratio = -here * inverse
        recip[level * LONS : (level + 1) * LONS, :] = inverse
        ratio[level * LONS : (level + 1) * LONS, :] = last_ratio
        below = here

    def solve(load_right, work, store):
        value = [jnp.zeros((LONS, 128), F32) for _ in range(variables)]
        lower = jnp.zeros((LONS, 128), F32)
        for level in range(levels):
            inverse = recip[level * LONS : (level + 1) * LONS, :]
            for var in range(variables):
                value[var] = (load_right(var, level) + lower * value[var]) * inverse
                work[level_rows(var, level), :] = value[var]
            lower = coefficient(level)
        for var in range(variables):
            store(var, levels - 1, value[var])
        for level in range(levels - 2, -1, -1):
            back = ratio[level * LONS : (level + 1) * LONS, :]
            for var in range(variables):
                value[var] = work[level_rows(var, level), :] - back * value[var]
                store(var, level, value[var])

    def load_cot(var, level):
        return (cot[level_rows(var, level), :] * live4).astype(BF16).astype(F32)

    def store_adj(var, level, value):
        adj[level_rows(var, level), :] = value

    solve(load_cot, adj, store_adj)
    for lon in range(LONS):
        adj_half[:, lon_cols(lon)] = adj[lon_rows(lon), :].astype(BF16)
    loads[7].wait()
    back_two[...] = lax.dot_general(w_out[...], adj_half[...], TN, preferred_element_type=F32)

    for copy in mix_copies:
        copy.wait_recv()
    lane = lax.broadcasted_iota(jnp.int32, (2 * LONS, 128), 1)
    mixes = [mix_in[0], mix[...], mix_in[1]]
    norths = [jnp.where(lane == 127, 0.0, m) for m in mixes]
    souths = [jnp.where(lane == 0, 0.0, pltpu.roll(m, 1, 1)) for m in mixes]

    def mix_row(tables, lon, offset):
        row = lon % LONS + offset
        return tables[lon // LONS + 1][row : row + 1]

    weights = []
    for lon in range(-1, LONS + 1):
        east = mix_row(mixes, lon, 0)
        west = mix_row(mixes, lon - 1, 0)
        north = mix_row(norths, lon, LONS)
        south = mix_row(souths, lon, LONS)
        weights.append((1.0 - east - west - north - south, east, west, north, south))

    def stencil(lon, west_val, own, east_val):
        centre, east, west, north, south = weights[lon + 1]
        return (
            centre * own
            + east * east_val
            + west * west_val
            + north * pltpu.roll(own, 127, 1)
            + south * pltpu.roll(own, 1, 1)
        )

    def advance(which, load_own, store):
        def load(lon):
            if lon < 0:
                return halo_in[which, 0, lon + 2].astype(F32)
            if lon >= LONS:
                return halo_in[which, 1, lon - LONS].astype(F32)
            return load_own(lon)

        for lon in range(-1, LONS + 1):
            mid_step[lon + 1] = stencil(lon, load(lon - 1), load(lon), load(lon + 1))
        for lon in range(LONS):
            store(lon, stencil(lon, mid_step[lon], mid_step[lon + 1], mid_step[lon + 2]))

    def load_prog(lon):
        return prog[lon_rows(lon), :]

    def store_moved(lon, value):
        moved[lon_rows(lon), :] = value
        x_half[:, lon_cols(lon)] = value.astype(BF16)

    for copy in halo_one:
        copy.wait_recv()
    advance(0, load_prog, store_moved)

    loads[8].wait()
    for block in range(units // CHUNK_ROWS):
        span = slice(block * CHUNK_ROWS, (block + 1) * CHUNK_ROWS)
        pre = jnp.dot(w_in[span, :], x_half[...], preferred_element_type=F32)
        sig = sigmoid(pre)
        act_one[span, :] = (pre * sig).astype(BF16)
        slope_one[span, :] = sig * (1.0 + pre * (1.0 - sig))

    def keep_chunk(chunk, first_row, value):
        for piece in range(value.shape[0] // rows):
            strip = value[piece * rows : (piece + 1) * rows, :]
            slot = first_row // rows + piece
            for side in range(2):
                block = strip[:, side * half : (side + 1) * half]
                part_f[side, chunk, slot] = block
                part_b[side, chunk, slot] = block.astype(BF16)

    s0 = []

    def send_s0(chunk):
        s0.append(
            send(
                part_b.at[1 - core, chunk],
                got0.at[chunk],
                s0_send.at[chunk],
                s0_recv.at[chunk],
                (y, partner),
            )
        )

    s1 = []

    def send_s1(chunk):
        s0[chunk].wait_recv()
        total = part_f[core, chunk] + got0[chunk].astype(F32)
        sum1_f[chunk] = total
        sum1_b[chunk] = total.astype(BF16)
        copies = ([], [])
        for step in range(1, n):
            copies[0].append(
                send(
                    sum1_b.at[chunk, at_x(step)],
                    got1.at[0, chunk, step - 1],
                    s1_send.at[0, chunk, step - 1],
                    s1_recv.at[0, chunk, step - 1],
                    (y, place(at_x(step), z, core)),
                )
            )
            copies[1].append(
                send(
                    sum1_b.at[chunk, n + at_y(step)],
                    got1.at[1, chunk, step - 1],
                    s1_send.at[1, chunk, step - 1],
                    s1_recv.at[1, chunk, step - 1],
                    (at_y(step), h),
                )
            )
        s1.append(copies)

    loads[9].wait()
    for block in range(units // CHUNK_ROWS):
        span = slice(block * CHUNK_ROWS, (block + 1) * CHUNK_ROWS)
        pre = jnp.dot(w_mid[span, :], act_one[...], preferred_element_type=F32)
        sig = sigmoid(pre)
        act_two[span, :] = (pre * sig).astype(BF16)
        delta = (back_two[span, :] * (sig * (1.0 + pre * (1.0 - sig)))).astype(BF16)
        delta_two[span, :] = delta
        keep_chunk(
            block, 0, lax.dot_general(delta, act_one[...], NT, preferred_element_type=F32)
        )
        send_s0(block)
        if block >= 1:
            send_s1(block - 1)

    keep_chunk(
        CHUNKS - 1,
        0,
        lax.dot_general(adj_half[...], act_two[...], NT, preferred_element_type=F32),
    )
    for block in range(units // CHUNK_ROWS):
        span = slice(block * CHUNK_ROWS, (block + 1) * CHUNK_ROWS)
        back = lax.dot_general(w_mid[:, span], delta_two[...], TN, preferred_element_type=F32)
        delta_one[span, :] = (back * slope_one[span, :]).astype(BF16)
    send_s1(CHUNKS - 2)
    grad_in = lax.dot_general(delta_one[...], x_half[...], NT, preferred_element_type=F32)
    keep_chunk(
        CHUNKS - 1,
        CHUNK_ROWS // 2,
        jnp.concatenate(
            [grad_in[b * 128 : (b + 1) * 128, :] for b in range(units // 128)], axis=1
        ),
    )
    send_s0(CHUNKS - 1)

    back_x = lax.dot_general(w_in[...], delta_one[...], TN, preferred_element_type=F32)
    for lon in range(LONS):
        fresh = adj[lon_rows(lon), :] + back_x[:, lon * 128 : (lon + 1) * 128]
        value = jnp.where(
            jnp.broadcast_to(live[lon : lon + 1], (fields, 128)) > 0.5,
            fresh.astype(BF16).astype(F32),
            cot[lon_rows(lon), :],
        )
        gfield[lon] = value
        halo_out[1, 1 - lon // 2, lon % 2] = value.astype(BF16)
    halo_two = send_halo(1)
    send_s1(CHUNKS - 1)

    tendency = jnp.dot(w_out[...], act_two[...], preferred_element_type=F32)
    for lon in range(LONS):
        forced[lon_rows(lon), :] = (
            x_half[:, lon_cols(lon)].astype(F32) + tendency[:, lon * 128 : (lon + 1) * 128]
        )

    def load_forced(var, level):
        return forced[level_rows(var, level), :]

    def store_state(var, level, value):
        here = level_rows(var, level)
        state_ref[here, :] = jnp.where(
            live4 > 0.5, value.astype(BF16).astype(F32), moved[here, :]
        )

    solve(load_forced, forced, store_state)

    own1 = (x, n + y)
    own2 = (y, x)
    s2 = []
    for chunk in range(CHUNKS):
        copies = ([], [])
        for colour in range(2):
            total = sum1_f[chunk, own1[colour]]
            for step in range(n - 1):
                s1[chunk][colour][step].wait_recv()
                total = total + got1[colour, chunk, step].astype(F32)
            for slot in range(n):
                block = total[:, slot * width : (slot + 1) * width]
                sum2_f[colour, chunk, slot] = block
                sum2_b[colour, chunk, slot] = block.astype(BF16)
            for step in range(1, n):
                target = at_y(step) if colour == 0 else at_x(step)
                peer = (target, h) if colour == 0 else (y, place(target, z, core))
                copies[colour].append(
                    send(
                        sum2_b.at[colour, chunk, target],
                        got2.at[colour, chunk, step - 1],
                        s2_send.at[colour, chunk, step - 1],
                        s2_recv.at[colour, chunk, step - 1],
                        peer,
                    )
                )
        s2.append(copies)

    def load_gfield(lon):
        return gfield[lon]

    def store_sgrad(lon, value):
        sgrad_ref[lon_rows(lon), :] = value

    for copy in halo_two:
        copy.wait_recv()
    advance(1, load_gfield, store_sgrad)

    strip = CHUNKS * rows
    if zrows * nz > 2 * strip:
        sum3_f[2 * strip :, :] = jnp.zeros((zrows * nz - 2 * strip, width), F32)
        sum3_b[2 * strip :, :] = jnp.zeros((zrows * nz - 2 * strip, width), BF16)
    for colour in range(2):
        for chunk in range(CHUNKS):
            total = sum2_f[colour, chunk, own2[colour]]
            for step in range(n - 1):
                s2[chunk][colour][step].wait_recv()
                total = total + got2[colour, chunk, step].astype(F32)
            first = colour * strip + chunk * rows
            sum3_f[first : first + rows, :] = total
            sum3_b[first : first + rows, :] = total.astype(BF16)

    def z_rows(zi):
        return pl.ds(pl.multiple_of(zi * zrows, 16), zrows)

    s3 = [
        send(
            sum3_b.at[z_rows(at_z(step)), :],
            got3.at[step - 1],
            s3_send.at[step - 1],
            s3_recv.at[step - 1],
            (y, place(x, at_z(step), core)),
        )
        for step in range(1, nz)
    ]
    total = sum3_f[z_rows(z), :]
    for step in range(nz - 1):
        s3[step].wait_recv()
        total = total + got3[step].astype(F32)
    owned[...] = (total * factor).astype(BF16)
    zfull[z_rows(z), :] = owned[...]
    g3 = [
        send(
            owned,
            zfull.at[z_rows(z), :],
            g3_send.at[step - 1],
            g3_recv.at[step - 1],
            (y, place(x, at_z(step), core)),
        )
        for step in range(1, nz)
    ]
    for copy in g3:
        copy.wait_recv()

    g2 = ([], [])
    for colour in range(2):
        band = pl.ds(colour * strip, strip)
        slot = (x, y) if colour == 0 else (y, x)
        full_ref[core, colour, slot[0], slot[1]] = zfull[band, :]
        for step in range(1, n):
            peer = (at_y(step), h) if colour == 0 else (y, place(at_x(step), z, core))
            g2[colour].append(
                send(
                    zfull.at[band, :],
                    full_ref.at[core, colour, slot[0], slot[1]],
                    g2_send.at[colour, step - 1],
                    g2_recv.at[colour, step - 1],
                    peer,
                )
            )
    g1 = ([], [])
    g0 = []

    def send_g0(colour, position, step):
        g0.append(
            send(
                full_ref.at[core, colour, position],
                full_ref.at[core, colour, position],
                g0_send.at[colour, step],
                g0_recv.at[colour, step],
                (y, partner),
            )
        )

    for colour in range(2):
        first = x if colour == 0 else y
        for copy in g2[colour]:
            copy.wait_recv()
        for step in range(1, n):
            peer = (y, place(at_x(step), z, core)) if colour == 0 else (at_y(step), h)
            g1[colour].append(
                send(
                    full_ref.at[core, colour, first],
                    full_ref.at[core, colour, first],
                    g1_send.at[colour, step - 1],
                    g1_recv.at[colour, step - 1],
                    peer,
                )
            )
        send_g0(colour, first, 0)
    for step in range(1, n):
        for colour in range(2):
            g1[colour][step - 1].wait_recv()
            first = x if colour == 0 else y
            send_g0(colour, (first + n - step) % n, step)
    for copy in g0:
        copy.wait_recv()
    for copy in sent:
        copy.wait_send()


def unscramble_kernel(half, full_ref, mid_ref, out_ref, in_ref):
    chunk = pl.program_id(0)
    _, colours, firsts, seconds, rows, width = full_ref.shape

    def strip(colour, first):
        return [
            full_ref[side, colour, first, second].astype(F32)
            for side in range(2)
            for second in range(seconds)
        ]

    @pl.when(chunk < CHUNKS - 1)
    def _():
        for colour in range(colours):
            for first in range(firsts):
                row = (colour * firsts + first) * rows
                for slot, block in enumerate(strip(colour, first)):
                    mid_ref[row : row + rows, slot * width : (slot + 1) * width] = block

    @pl.when(chunk == CHUNKS - 1)
    def _():
        for first in range(firsts):
            row = first * rows
            for slot, block in enumerate(strip(0, first)):
                out_ref[row : row + rows, slot * width : (slot + 1) * width] = block
            for slot, block in enumerate(strip(1, first)):
                for part in range(width // 128):
                    start = (slot * (width // 128) + part) * 128 + row
                    in_ref[start : start + rows, :] = block[:, part * 128 : (part + 1) * 128]


def per_device(
    nz, prognostic, diffusivity, mixing, cotangent, tile_cols, pad_mask, tile_count, w_in, w_mid, w_out
):
    n = lax.axis_size("ens")
    fields = prognostic.shape[1]
    levels = diffusivity.shape[1]
    units = w_mid.shape[0]
    half = units // 2
    rows = CHUNK_ROWS // (2 * n)
    width = half // n
    tiles = tile_cols.shape[2]
    zrows = -(-2 * CHUNKS * rows // (16 * nz)) * 16
    flat = (fields * LONS, 128)
    factor = 1.0 / math.sqrt(n * lax.axis_size("horiz") * LONS * 128)
    dma = pltpu.SemaphoreType.DMA
    vm = pltpu.VMEM
    any_spec = pl.BlockSpec(memory_space=pl.ANY)
    vmem_spec = pl.BlockSpec(memory_space=pltpu.VMEM)
    state, sgrad, full = pl.pallas_call(
        functools.partial(window_kernel, (n, nz, levels, fields // levels), factor),
        out_shape=(
            jax.ShapeDtypeStruct(flat, F32),
            jax.ShapeDtypeStruct(flat, F32),
            jax.ShapeDtypeStruct((2, 2, n, n, CHUNKS * rows, width), BF16),
        ),
        in_specs=[any_spec] * 10,
        out_specs=(vmem_spec, vmem_spec, vmem_spec),
        scratch_shapes=[
            vm(flat, F32),
            vm((levels * LONS, 128), F32),
            vm((2 * LONS, 128), F32),
            vm(flat, F32),
            vm((tiles, 1, 128), jnp.int32),
            vm((tiles, 1, 128), jnp.int32),
            pltpu.SMEM((1, 1), jnp.int32),
            vm(w_in.shape, BF16),
            vm(w_mid.shape, BF16),
            vm(w_out.shape, BF16),
            vm((2, 2, 2, fields, 128), BF16),
            vm((2, 2, 2, fields, 128), BF16),
            vm((2, 2 * LONS, 128), F32),
            vm((LONS + 2, fields, 128), F32),
            vm(flat, F32),
            vm((levels * LONS, 128), F32),
            vm((levels * LONS, 128), F32),
            vm(flat, F32),
            vm(flat, F32),
            vm((LONS, fields, 128), F32),
            vm((fields, LONS * 128), BF16),
            vm((fields, LONS * 128), BF16),
            vm((units, LONS * 128), F32),
            vm((units, LONS * 128), F32),
            vm((units, LONS * 128), BF16),
            vm((units, LONS * 128), BF16),
            vm((units, LONS * 128), BF16),
            vm((units, LONS * 128), BF16),
            vm((2, CHUNKS, 2 * n, rows, half), F32),
            vm((2, CHUNKS, 2 * n, rows, half), BF16),
            vm((CHUNKS, 2 * n, rows, half), BF16),
            vm((CHUNKS, 2 * n, rows, half), F32),
            vm((CHUNKS, 2 * n, rows, half), BF16),
            vm((2, CHUNKS, n - 1, rows, half), BF16),
            vm((2, CHUNKS, n, rows, width), F32),
            vm((2, CHUNKS, n, rows, width), BF16),
            vm((2, CHUNKS, n - 1, rows, width), BF16),
            vm((zrows * nz, width), F32),
            vm((zrows * nz, width), BF16),
            vm((nz - 1, zrows, width), BF16),
            vm((zrows, width), BF16),
            vm((zrows * nz, width), BF16),
            dma((10,)),
            dma((3, 2)),
            dma((3, 2)),
            dma((CHUNKS,)),
            dma((CHUNKS,)),
            dma((2, CHUNKS, n - 1)),
            dma((2, CHUNKS, n - 1)),
            dma((2, CHUNKS, n - 1)),
            dma((2, CHUNKS, n - 1)),
            dma((nz - 1,)),
            dma((nz - 1,)),
            dma((nz - 1,)),
            dma((nz - 1,)),
            dma((2, n - 1)),
            dma((2, n - 1)),
            dma((2, n - 1)),
            dma((2, n - 1)),
            dma((2, n)),
            dma((2, n)),
        ],
        compiler_params=pltpu.CompilerParams(
            collective_id=0, has_side_effects=True, vmem_limit_bytes=60 * 1024 * 1024
        ),
    )(
        prognostic.reshape(flat),
        diffusivity.reshape(levels * LONS, 128),
        mixing.reshape(2 * LONS, 128),
        cotangent.reshape(flat),
        tile_cols.reshape(tiles, 1, 128),
        pad_mask.reshape(tiles, 1, 128),
        tile_count,
        w_in,
        w_mid,
        w_out,
    )
    grad_mid, grad_out, grad_in = pl.pallas_call(
        functools.partial(unscramble_kernel, half),
        grid=(CHUNKS,),
        out_shape=(
            jax.ShapeDtypeStruct(w_mid.shape, F32),
            jax.ShapeDtypeStruct(w_out.shape, F32),
            jax.ShapeDtypeStruct(w_in.shape, F32),
        ),
        in_specs=[pl.BlockSpec((2, 2, n, n, rows, width), lambda k: (0, 0, 0, 0, k, 0))],
        out_specs=(
            pl.BlockSpec((CHUNK_ROWS, units), lambda k: (jnp.minimum(k, CHUNKS - 2), 0)),
            pl.BlockSpec(w_out.shape, lambda k: (0, 0)),
            pl.BlockSpec(w_in.shape, lambda k: (0, 0)),
        ),
    )(full)
    return (
        state.reshape(prognostic.shape),
        sgrad.reshape(prognostic.shape),
        grad_in,
        grad_mid,
        grad_out,
    )


def solution(mesh):
    placed = (
        P("ens", None, "horiz", None),
        P("ens", None, "horiz", None),
        P(None, "horiz", None),
        P("ens", None, "horiz", None),
        P("ens", "horiz", None, None),
        P("ens", "horiz", None, None),
        P("ens", "horiz"),
        P(),
        P(),
        P(),
    )
    nz = mesh.shape["horiz"] // (2 * mesh.shape["ens"])
    return jax.shard_map(
        functools.partial(per_device, nz),
        mesh=mesh,
        in_specs=placed,
        out_specs=(P("ens", None, "horiz", None), P("ens", None, "horiz", None), P(), P(), P()),
        check_vma=False,
    )
```

time: 406 us -> 70.3 us (0.17)
  waiting for transfers between devices: 293 us -> 0 us
  Pallas kernels: 0 us -> 67.3 us
  starting transfers between devices: 37 us -> 0 us
  local copies, waits for them, and re-layouts: 25.1 us -> 1.41 us
  other arithmetic: 19.1 us -> 0 us
  between operations: 15.1 us -> 1.31 us
  matrix products: 8.44 us -> 0 us
  loops' own time: 7.49 us -> 0 us
    psum x1 -> x0, waiting for transfers between devices: 285 us -> none  [per_device(): lax.psum((grad_sums[0], grad_sums[1], grad_sums[2]), ('ens', 'horiz'))]
    pallas_call x0 -> x2, Pallas kernels: none -> 67.3 us  [the longest x1 61.7 us: per_device(): pl.pallas_call(functools.partial(window_kernel, (n, nz, levels, fields //...]
    ppermute x9 -> x0, starting transfers between devices: 36.9 us -> none  [the longest x4 22.9 us: with_halo(): lax.ppermute(lax.slice_in_dim(block, block.shape[dim] - width, None, axis...]
    mul x7 -> x0, other arithmetic: 9.13 us -> none  [the longest x1 5.12 us: per_device(): summed[1] * factor]
    dot_general x9 -> x0, matrix products: 8.44 us -> none  [the longest x1 2.43 us: column_physics(): pre_two = jnp.dot(w_mid, act_one, preferred_element_type=jnp.float32)]
    another operation x5 -> x0, loops' own time: 7.49 us -> none  [the longest x1 3.55 us: run_tiles(): finished = lax.fori_loop(0, live_count, visit_tile, start_state)]
    ppermute x9 -> x0, waiting for transfers between devices: 7.43 us -> none  [the longest x4 4.91 us: with_halo(): lax.ppermute(lax.slice_in_dim(block, block.shape[dim] - width, None, axis...]
  transfers between devices with their start and end apart: 10 -> 0, of which waited for: 4 -> 0; matrix products, arithmetic and copies ran while one was open for 4% -> 0% of each run, Pallas kernels for 0% -> 0%
where the time goes in v1:
time: 70.3 us; the launch traced here: 70.1 us
  Pallas kernels  67.3 us (96%)
  local copies, waits for them, and re-layouts  1.41 us (2%)
  between operations  1.31 us (2%)
    pallas_call x1, Pallas kernels, per_device(): pl.pallas_call(functools.partial(window_kernel, (n, nz, levels, fields //...  61.7 us
    pallas_call x1, Pallas kernels, per_device(): pl.pallas_call(functools.partial(unscramble_kernel, half), grid=(CHUNKS,)...  5.65 us
    unnamed x6, local copies, waits for them, and re-layouts  1.41 us

profile of v1, /device:TPU:1, one launch (start us, length us, event | category | flops | bytes accessed | tf_op | source)
XLA Modules:
  0.0 70.1 jit_solution(277867388873749908)
XLA Ops:
  1.3 61.7 %shard_map.137 = (f32[512,128]{1,0:T(8,128)}, f32[512,128]{1,0:T(8,128)}, bf16[2,2,4,4,160,128]{5,4,3,2,1,0:T(8,128)(2,1)}) custom-call(f32[512,128]{1,0:T(8,128)} %bitcast.8, f32[128,128]{1,0:T(8,128)} %bitcast.12, f32[8,128]{1,0:T(8,128)} %bitcast.13, f32[512,128]{1,0:T(8,128)} %bitcast.9, s32[3,1,128]{2,1,0:T(1,128)} %bitcast.14, s32[3,1,128]{2,1,0:T(1,128)} %bitcast.15, ...), custom_call_target="tpu_custom_call" | custom-call | tf_op jit(solution)/shard_map/pallas_call | solution.py:641
  63.0 0.0 copy-start.1
  63.0 0.0 copy-start
  63.0 5.6 %shard_map.138 = (f32[1024,1024]{1,0:T(8,128)}, f32[128,1024]{1,0:T(8,128)}, f32[1024,128]{1,0:T(8,128)}) custom-call(bf16[2,2,4,4,160,128]{5,4,3,2,1,0:T(8,128)(2,1)} %get-tuple-element.13.full_ref), custom_call_target="tpu_custom_call" | custom-call | tf_op jit(solution)/shard_map/pallas_call | solution.py:728
  68.7 0.0 copy-done.1
  68.7 0.7 %copy.18 = f32[1,128,4,128]{3,2,1,0:T(4,128)} copy(f32[1,128,4,128]{3,2,1,0:T(4,128)S(1)} %bitcast.11) | data formatting | bytes 524288
  69.4 0.0 copy-done
  69.4 0.7 %copy.19 = f32[1,128,4,128]{3,2,1,0:T(4,128)} copy(f32[1,128,4,128]{3,2,1,0:T(4,128)S(1)} %bitcast.10) | data formatting | bytes 524288
Async XLA Ops:
  63.0 5.7 %copy-start.1 = (f32[512,128]{1,0:T(8,128)S(1)}, f32[512,128]{1,0:T(8,128)}, u32[]{:S(2)}) copy-start(f32[512,128]{1,0:T(8,128)} %get-tuple-element.11) | copy-start | bytes 786436
  63.0 6.4 %copy-start = (f32[512,128]{1,0:T(8,128)S(1)}, f32[512,128]{1,0:T(8,128)}, u32[]{:S(2)}) copy-start(f32[512,128]{1,0:T(8,128)} %get-tuple-element.12) | copy-start | bytes 786436

commit v2 on v1

--- a/solution.py
+++ b/solution.py
@@ -11,6 +11,7 @@
 MESH = pl.DeviceIdType.MESH
 LONS = 4
 CHUNKS = 5
+GROUPS = ((0, 1), (2, 3), (4,))
 CHUNK_ROWS = 256
 F32 = jnp.float32
 BF16 = jnp.bfloat16
@@ -116,7 +117,7 @@
     pieces = 2 * n
     rows = CHUNK_ROWS // pieces
     width = half // n
-    zrows = owned.shape[0]
+    zrows = owned.shape[1]
 
     def at_x(step):
         return (x + step) % n
@@ -200,13 +201,6 @@
     for lon in range(LONS):
         halo_out[0, 1 - lon // 2, lon % 2] = prog[lon_rows(lon), :].astype(BF16)
     loads[1].wait()
-    pl.semaphore_wait(barrier, len(greeted))
-    halo_one = send_halo(0)
-    mix_copies = [
-        send(mix, mix_in.at[0], halo_send.at[2, 0], halo_recv.at[2, 0], (y, right)),
-        send(mix, mix_in.at[1], halo_send.at[2, 1], halo_recv.at[2, 1], (y, left)),
-    ]
-
     for copy in loads[2:7]:
         copy.wait()
     lon_of = lax.broadcasted_iota(jnp.int32, (16, 128), 0)
@@ -242,7 +236,7 @@
         ratio[level * LONS : (level + 1) * LONS, :] = last_ratio
         below = here
 
-    def solve(load_right, work, store):
+    def sweep_down(load_right, work):
         value = [jnp.zeros((LONS, 128), F32) for _ in range(variables)]
         lower = jnp.zeros((LONS, 128), F32)
         for level in range(levels):
@@ -251,6 +245,9 @@
                 value[var] = (load_right(var, level) + lower * value[var]) * inverse
                 work[level_rows(var, level), :] = value[var]
             lower = coefficient(level)
+
+    def sweep_up(work, store):
+        value = [work[level_rows(var, levels - 1), :] for var in range(variables)]
         for var in range(variables):
             store(var, levels - 1, value[var])
         for level in range(levels - 2, -1, -1):
@@ -265,7 +262,14 @@
     def store_adj(var, level, value):
         adj[level_rows(var, level), :] = value
 
-    solve(load_cot, adj, store_adj)
+    sweep_down(load_cot, adj)
+    pl.semaphore_wait(barrier, len(greeted))
+    halo_one = send_halo(0)
+    mix_copies = [
+        send(mix, mix_in.at[0], halo_send.at[2, 0], halo_recv.at[2, 0], (y, right)),
+        send(mix, mix_in.at[1], halo_send.at[2, 1], halo_recv.at[2, 1], (y, left)),
+    ]
+    sweep_up(adj, store_adj)
     for lon in range(LONS):
         adj_half[:, lon_cols(lon)] = adj[lon_rows(lon), :].astype(BF16)
     loads[7].wait()
@@ -332,21 +336,37 @@
         act_one[span, :] = (pre * sig).astype(BF16)
         slope_one[span, :] = sig * (1.0 + pre * (1.0 - sig))
 
-    def keep_chunk(chunk, first_row, value):
-        for piece in range(value.shape[0] // rows):
-            strip = value[piece * rows : (piece + 1) * rows, :]
-            slot = first_row // rows + piece
-            for side in range(2):
-                block = strip[:, side * half : (side + 1) * half]
-                part_f[side, chunk, slot] = block
-                part_b[side, chunk, slot] = block.astype(BF16)
+    other = 1 - core
+
+    def side_rows(side):
+        return pl.ds(pl.multiple_of(side * half, half), half)
+
+    def chunk_half(chunk, side):
+        if chunk < CHUNKS - 1:
+            left_side = delta_two[chunk * CHUNK_ROWS : (chunk + 1) * CHUNK_ROWS, :]
+            value = lax.dot_general(
+                left_side, act_one[side_rows(side), :], NT, preferred_element_type=F32
+            )
+        else:
+            top = lax.dot_general(
+                adj_half[...], act_two[side_rows(side), :], NT, preferred_element_type=F32
+            )
+            low = lax.dot_general(
+                delta_one[side_rows(side), :], x_half[...], NT, preferred_element_type=F32
+            )
+            low = jnp.concatenate(
+                [low[b * 128 : (b + 1) * 128, :] for b in range(half // 128)], axis=1
+            )
+            value = jnp.concatenate([top, low], axis=0)
+        return value.reshape(pieces, rows, half)
 
     s0 = []
 
     def send_s0(chunk):
+        part_b[chunk] = chunk_half(chunk, other).astype(BF16)
         s0.append(
             send(
-                part_b.at[1 - core, chunk],
+                part_b.at[chunk],
                 got0.at[chunk],
                 s0_send.at[chunk],
                 s0_recv.at[chunk],
@@ -358,7 +378,7 @@
 
     def send_s1(chunk):
         s0[chunk].wait_recv()
-        total = part_f[core, chunk] + got0[chunk].astype(F32)
+        total = part_f[chunk] + got0[chunk].astype(F32)
         sum1_f[chunk] = total
         sum1_b[chunk] = total.astype(BF16)
         copies = ([], [])
@@ -391,33 +411,21 @@
         act_two[span, :] = (pre * sig).astype(BF16)
         delta = (back_two[span, :] * (sig * (1.0 + pre * (1.0 - sig)))).astype(BF16)
         delta_two[span, :] = delta
-        keep_chunk(
-            block, 0, lax.dot_general(delta, act_one[...], NT, preferred_element_type=F32)
-        )
-        send_s0(block)
-        if block >= 1:
-            send_s1(block - 1)
-
-    keep_chunk(
-        CHUNKS - 1,
-        0,
-        lax.dot_general(adj_half[...], act_two[...], NT, preferred_element_type=F32),
-    )
+
+    def keep_half(chunk):
+        part_f[chunk] = chunk_half(chunk, core)
+
+    for chunk in range(CHUNKS - 1):
+        send_s0(chunk)
+    for chunk in range(CHUNKS - 1):
+        keep_half(chunk)
+        send_s1(chunk)
     for block in range(units // CHUNK_ROWS):
         span = slice(block * CHUNK_ROWS, (block + 1) * CHUNK_ROWS)
         back = lax.dot_general(w_mid[:, span], delta_two[...], TN, preferred_element_type=F32)
         delta_one[span, :] = (back * slope_one[span, :]).astype(BF16)
-    send_s1(CHUNKS - 2)
-    grad_in = lax.dot_general(delta_one[...], x_half[...], NT, preferred_element_type=F32)
-    keep_chunk(
-        CHUNKS - 1,
-        CHUNK_ROWS // 2,
-        jnp.concatenate(
-            [grad_in[b * 128 : (b + 1) * 128, :] for b in range(units // 128)], axis=1
-        ),
-    )
     send_s0(CHUNKS - 1)
-
+    keep_half(CHUNKS - 1)
     back_x = lax.dot_general(w_in[...], delta_one[...], TN, preferred_element_type=F32)
     for lon in range(LONS):
         fresh = adj[lon_rows(lon), :] + back_x[:, lon * 128 : (lon + 1) * 128]
@@ -431,50 +439,154 @@
     halo_two = send_halo(1)
     send_s1(CHUNKS - 1)
 
-    tendency = jnp.dot(w_out[...], act_two[...], preferred_element_type=F32)
-    for lon in range(LONS):
-        forced[lon_rows(lon), :] = (
-            x_half[:, lon_cols(lon)].astype(F32) + tendency[:, lon * 128 : (lon + 1) * 128]
-        )
-
-    def load_forced(var, level):
-        return forced[level_rows(var, level), :]
-
-    def store_state(var, level, value):
-        here = level_rows(var, level)
-        state_ref[here, :] = jnp.where(
-            live4 > 0.5, value.astype(BF16).astype(F32), moved[here, :]
-        )
-
-    solve(load_forced, forced, store_state)
+    def tail_solve():
+        tendency = jnp.dot(w_out[...], act_two[...], preferred_element_type=F32)
+        for lon in range(LONS):
+            forced[lon_rows(lon), :] = (
+                x_half[:, lon_cols(lon)].astype(F32) + tendency[:, lon * 128 : (lon + 1) * 128]
+            )
+
+        def load_forced(var, level):
+            return forced[level_rows(var, level), :]
+
+        def store_state(var, level, value):
+            here = level_rows(var, level)
+            state_ref[here, :] = jnp.where(
+                live4 > 0.5, value.astype(BF16).astype(F32), moved[here, :]
+            )
+
+        sweep_down(load_forced, forced)
+        sweep_up(forced, store_state)
 
     own1 = (x, n + y)
     own2 = (y, x)
-    s2 = []
-    for chunk in range(CHUNKS):
-        copies = ([], [])
-        for colour in range(2):
-            total = sum1_f[chunk, own1[colour]]
-            for step in range(n - 1):
-                s1[chunk][colour][step].wait_recv()
-                total = total + got1[colour, chunk, step].astype(F32)
-            for slot in range(n):
-                block = total[:, slot * width : (slot + 1) * width]
-                sum2_f[colour, chunk, slot] = block
-                sum2_b[colour, chunk, slot] = block.astype(BF16)
-            for step in range(1, n):
-                target = at_y(step) if colour == 0 else at_x(step)
-                peer = (target, h) if colour == 0 else (y, place(target, z, core))
-                copies[colour].append(
-                    send(
-                        sum2_b.at[colour, chunk, target],
+    s2, s3, g3, g2, g1, g0 = {}, {}, {}, {}, {}, {}
+
+    def first_peer(colour, step):
+        return (y, place(at_x(step), z, core)) if colour == 0 else (at_y(step), h)
+
+    def second_peer(colour, step):
+        return (at_y(step), h) if colour == 0 else (y, place(at_x(step), z, core))
+
+    def send_s2(group):
+        for chunk in GROUPS[group]:
+            for colour in range(2):
+                total = sum1_f[chunk, own1[colour]]
+                for step in range(n - 1):
+                    s1[chunk][colour][step].wait_recv()
+                    total = total + got1[colour, chunk, step].astype(F32)
+                for slot in range(n):
+                    block = total[:, slot * width : (slot + 1) * width]
+                    sum2_f[colour, chunk, slot] = block
+                    sum2_b[colour, chunk, slot] = block.astype(BF16)
+                for step in range(1, n):
+                    s2[chunk, colour, step] = send(
+                        sum2_b.at[colour, chunk, at_y(step) if colour == 0 else at_x(step)],
                         got2.at[colour, chunk, step - 1],
                         s2_send.at[colour, chunk, step - 1],
                         s2_recv.at[colour, chunk, step - 1],
-                        peer,
+                        second_peer(colour, step),
                     )
+
+    def z_rows(zi):
+        return pl.ds(pl.multiple_of(zi * zrows, 16), zrows)
+
+    def z_peer(step):
+        return (y, place(x, at_z(step), core))
+
+    def send_s3(group):
+        chunks = GROUPS[group]
+        filled = 2 * len(chunks) * rows
+        if zrows * nz > filled:
+            sum3_f[group, filled:, :] = jnp.zeros((zrows * nz - filled, width), F32)
+            sum3_b[group, filled:, :] = jnp.zeros((zrows * nz - filled, width), BF16)
+        for colour in range(2):
+            for slot, chunk in enumerate(chunks):
+                total = sum2_f[colour, chunk, own2[colour]]
+                for step in range(1, n):
+                    s2[chunk, colour, step].wait_recv()
+                    total = total + got2[colour, chunk, step - 1].astype(F32)
+                start = (colour * len(chunks) + slot) * rows
+                sum3_f[group, start : start + rows, :] = total
+                sum3_b[group, start : start + rows, :] = total.astype(BF16)
+        for step in range(1, nz):
+            s3[group, step] = send(
+                sum3_b.at[group, z_rows(at_z(step)), :],
+                got3.at[group, step - 1],
+                s3_send.at[group, step - 1],
+                s3_recv.at[group, step - 1],
+                z_peer(step),
+            )
+
+    def send_g3(group):
+        total = sum3_f[group, z_rows(z), :]
+        for step in range(1, nz):
+            s3[group, step].wait_recv()
+            total = total + got3[group, step - 1].astype(F32)
+        mine = (total * factor).astype(BF16)
+        owned[group] = mine
+        zfull[group, z_rows(z), :] = mine
+        for step in range(1, nz):
+            g3[group, step] = send(
+                owned.at[group],
+                zfull.at[group, z_rows(z), :],
+                g3_send.at[group, step - 1],
+                g3_recv.at[group, step - 1],
+                z_peer(step),
+            )
+
+    def group_rows(group):
+        return pl.ds(GROUPS[group][0] * rows, len(GROUPS[group]) * rows)
+
+    def send_g2(group):
+        for step in range(1, nz):
+            g3[group, step].wait_recv()
+        band = len(GROUPS[group]) * rows
+        for colour in range(2):
+            slot = (x, y) if colour == 0 else (y, x)
+            source = pl.ds(colour * band, band)
+            full_ref[core, colour, slot[0], slot[1], group_rows(group), :] = zfull[group, source, :]
+            for step in range(1, n):
+                g2[group, colour, step] = send(
+                    zfull.at[group, source, :],
+                    full_ref.at[core, colour, slot[0], slot[1], group_rows(group), :],
+                    g2_send.at[group, colour, step - 1],
+                    g2_recv.at[group, colour, step - 1],
+                    second_peer(colour, step),
                 )
-        s2.append(copies)
+
+    def send_g0(group, colour, position, step):
+        piece = full_ref.at[core, colour, position, :, group_rows(group), :]
+        g0[group, colour, step] = send(
+            piece,
+            piece,
+            g0_send.at[group, colour, step],
+            g0_recv.at[group, colour, step],
+            (y, partner),
+        )
+
+    def send_g1(group):
+        for colour in range(2):
+            first = x if colour == 0 else y
+            for step in range(1, n):
+                g2[group, colour, step].wait_recv()
+            piece = full_ref.at[core, colour, first, :, group_rows(group), :]
+            for step in range(1, n):
+                g1[group, colour, step] = send(
+                    piece,
+                    piece,
+                    g1_send.at[group, colour, step - 1],
+                    g1_recv.at[group, colour, step - 1],
+                    first_peer(colour, step),
+                )
+            send_g0(group, colour, first, 0)
+
+    def forward(group):
+        for step in range(1, n):
+            for colour in range(2):
+                g1[group, colour, step].wait_recv()
+                first = x if colour == 0 else y
+                send_g0(group, colour, (first + n - step) % n, step)
 
     def load_gfield(lon):
         return gfield[lon]
@@ -482,142 +594,77 @@
     def store_sgrad(lon, value):
         sgrad_ref[lon_rows(lon), :] = value
 
+    send_s2(0)
+    tail_solve()
+    send_s3(0)
+    send_s2(1)
     for copy in halo_two:
         copy.wait_recv()
     advance(1, load_gfield, store_sgrad)
-
-    strip = CHUNKS * rows
-    if zrows * nz > 2 * strip:
-        sum3_f[2 * strip :, :] = jnp.zeros((zrows * nz - 2 * strip, width), F32)
-        sum3_b[2 * strip :, :] = jnp.zeros((zrows * nz - 2 * strip, width), BF16)
-    for colour in range(2):
-        for chunk in range(CHUNKS):
-            total = sum2_f[colour, chunk, own2[colour]]
-            for step in range(n - 1):
-                s2[chunk][colour][step].wait_recv()
-                total = total + got2[colour, chunk, step].astype(F32)
-            first = colour * strip + chunk * rows
-            sum3_f[first : first + rows, :] = total
-            sum3_b[first : first + rows, :] = total.astype(BF16)
-
-    def z_rows(zi):
-        return pl.ds(pl.multiple_of(zi * zrows, 16), zrows)
-
-    s3 = [
-        send(
-            sum3_b.at[z_rows(at_z(step)), :],
-            got3.at[step - 1],
-            s3_send.at[step - 1],
-            s3_recv.at[step - 1],
-            (y, place(x, at_z(step), core)),
-        )
-        for step in range(1, nz)
-    ]
-    total = sum3_f[z_rows(z), :]
-    for step in range(nz - 1):
-        s3[step].wait_recv()
-        total = total + got3[step].astype(F32)
-    owned[...] = (total * factor).astype(BF16)
-    zfull[z_rows(z), :] = owned[...]
-    g3 = [
-        send(
-            owned,
-            zfull.at[z_rows(z), :],
-            g3_send.at[step - 1],
-            g3_recv.at[step - 1],
-            (y, place(x, at_z(step), core)),
-        )
-        for step in range(1, nz)
-    ]
-    for copy in g3:
-        copy.wait_recv()
-
-    g2 = ([], [])
-    for colour in range(2):
-        band = pl.ds(colour * strip, strip)
-        slot = (x, y) if colour == 0 else (y, x)
-        full_ref[core, colour, slot[0], slot[1]] = zfull[band, :]
-        for step in range(1, n):
-            peer = (at_y(step), h) if colour == 0 else (y, place(at_x(step), z, core))
-            g2[colour].append(
-                send(
-                    zfull.at[band, :],
-                    full_ref.at[core, colour, slot[0], slot[1]],
-                    g2_send.at[colour, step - 1],
-                    g2_recv.at[colour, step - 1],
-                    peer,
-                )
-            )
-    g1 = ([], [])
-    g0 = []
-
-    def send_g0(colour, position, step):
-        g0.append(
-            send(
-                full_ref.at[core, colour, position],
-                full_ref.at[core, colour, position],
-                g0_send.at[colour, step],
-                g0_recv.at[colour, step],
-                (y, partner),
-            )
-        )
-
-    for colour in range(2):
-        first = x if colour == 0 else y
-        for copy in g2[colour]:
-            copy.wait_recv()
-        for step in range(1, n):
-            peer = (y, place(at_x(step), z, core)) if colour == 0 else (at_y(step), h)
-            g1[colour].append(
-                send(
-                    full_ref.at[core, colour, first],
-                    full_ref.at[core, colour, first],
-                    g1_send.at[colour, step - 1],
-                    g1_recv.at[colour, step - 1],
-                    peer,
-                )
-            )
-        send_g0(colour, first, 0)
-    for step in range(1, n):
-        for colour in range(2):
-            g1[colour][step - 1].wait_recv()
-            first = x if colour == 0 else y
-            send_g0(colour, (first + n - step) % n, step)
-    for copy in g0:
+    send_s2(2)
+    send_s3(1)
+    send_g3(0)
+    send_s3(2)
+    send_g3(1)
+    send_g2(0)
+    send_g3(2)
+    send_g1(0)
+    send_g2(1)
+    send_g2(2)
+    send_g1(1)
+    forward(0)
+    send_g1(2)
+    forward(1)
+    forward(2)
+    for copy in g0.values():
         copy.wait_recv()
     for copy in sent:
         copy.wait_send()
 
 
-def unscramble_kernel(half, full_ref, mid_ref, out_ref, in_ref):
-    chunk = pl.program_id(0)
-    _, colours, firsts, seconds, rows, width = full_ref.shape
-
-    def strip(colour, first):
-        return [
-            full_ref[side, colour, first, second].astype(F32)
-            for side in range(2)
-            for second in range(seconds)
-        ]
-
-    @pl.when(chunk < CHUNKS - 1)
-    def _():
+def unscramble_kernel(
+    half, state_ref, sgrad_ref, full_ref, state_out, sgrad_out, mid_out, out_out, in_out, mid, out, inn, sems
+):
+    _, colours, firsts, seconds, strip, width = full_ref.shape
+    rows = strip // CHUNKS
+    copies = []
+
+    def emit(src, dst):
+        copy = pltpu.make_async_copy(src, dst, sems.at[len(copies)])
+        copy.start()
+        copies.append(copy)
+
+    emit(state_ref, state_out)
+    emit(sgrad_ref, sgrad_out)
+    for chunk in range(CHUNKS):
         for colour in range(colours):
             for first in range(firsts):
                 row = (colour * firsts + first) * rows
-                for slot, block in enumerate(strip(colour, first)):
-                    mid_ref[row : row + rows, slot * width : (slot + 1) * width] = block
-
-    @pl.when(chunk == CHUNKS - 1)
-    def _():
-        for first in range(firsts):
-            row = first * rows
-            for slot, block in enumerate(strip(0, first)):
-                out_ref[row : row + rows, slot * width : (slot + 1) * width] = block
-            for slot, block in enumerate(strip(1, first)):
-                for part in range(width // 128):
-                    start = (slot * (width // 128) + part) * 128 + row
-                    in_ref[start : start + rows, :] = block[:, part * 128 : (part + 1) * 128]
+                for slot in range(2 * seconds):
+                    block = full_ref[
+                        slot // seconds,
+                        colour,
+                        first,
+                        slot % seconds,
+                        chunk * rows : (chunk + 1) * rows,
+                        :,
+                    ].astype(F32)
+                    lanes = slice(slot * width, (slot + 1) * width)
+                    if chunk < CHUNKS - 1:
+                        mid[chunk * CHUNK_ROWS + row : chunk * CHUNK_ROWS + row + rows, lanes] = block
+                    elif colour == 0:
+                        out[row : row + rows, lanes] = block
+                    else:
+                        for part in range(width // 128):
+                            start = slot * width + part * 128 + first * rows
+                            inn[start : start + rows, :] = block[:, part * 128 : (part + 1) * 128]
+        if chunk < CHUNKS - 1:
+            span = pl.ds(chunk * CHUNK_ROWS, CHUNK_ROWS)
+            emit(mid.at[span, :], mid_out.at[span, :])
+    emit(out, out_out)
+    emit(inn, in_out)
+    for copy in copies:
+        copy.wait()
 
 
 def per_device(
@@ -631,13 +678,29 @@
     rows = CHUNK_ROWS // (2 * n)
     width = half // n
     tiles = tile_cols.shape[2]
-    zrows = -(-2 * CHUNKS * rows // (16 * nz)) * 16
+    groups = len(GROUPS)
+    zrows = -(-2 * max(len(g) for g in GROUPS) * rows // (16 * nz)) * 16
     flat = (fields * LONS, 128)
     factor = 1.0 / math.sqrt(n * lax.axis_size("horiz") * LONS * 128)
     dma = pltpu.SemaphoreType.DMA
     vm = pltpu.VMEM
-    any_spec = pl.BlockSpec(memory_space=pl.ANY)
+    any_spec = pl.BlockSpec(memory_space=pltpu.HBM)
     vmem_spec = pl.BlockSpec(memory_space=pltpu.VMEM)
+    operands = [
+        prognostic.reshape(flat),
+        diffusivity.reshape(levels * LONS, 128),
+        mixing.reshape(2 * LONS, 128),
+        cotangent.reshape(flat),
+        tile_cols.reshape(tiles, 1, 128),
+        pad_mask.reshape(tiles, 1, 128),
+        tile_count,
+        w_in,
+        w_mid,
+        w_out,
+    ]
+    operands = [
+        v if v.size == 1 else pltpu.with_memory_space_constraint(v, pltpu.HBM) for v in operands
+    ]
     state, sgrad, full = pl.pallas_call(
         functools.partial(window_kernel, (n, nz, levels, fields // levels), factor),
         out_shape=(
@@ -676,8 +739,8 @@
             vm((units, LONS * 128), BF16),
             vm((units, LONS * 128), BF16),
             vm((units, LONS * 128), BF16),
-            vm((2, CHUNKS, 2 * n, rows, half), F32),
-            vm((2, CHUNKS, 2 * n, rows, half), BF16),
+            vm((CHUNKS, 2 * n, rows, half), F32),
+            vm((CHUNKS, 2 * n, rows, half), BF16),
             vm((CHUNKS, 2 * n, rows, half), BF16),
             vm((CHUNKS, 2 * n, rows, half), F32),
             vm((CHUNKS, 2 * n, rows, half), BF16),
@@ -685,11 +748,11 @@
             vm((2, CHUNKS, n, rows, width), F32),
             vm((2, CHUNKS, n, rows, width), BF16),
             vm((2, CHUNKS, n - 1, rows, width), BF16),
-            vm((zrows * nz, width), F32),
-            vm((zrows * nz, width), BF16),
-            vm((nz - 1, zrows, width), BF16),
-            vm((zrows, width), BF16),
-            vm((zrows * nz, width), BF16),
+            vm((groups, zrows * nz, width), F32),
+            vm((groups, zrows * nz, width), BF16),
+            vm((groups, nz - 1, zrows, width), BF16),
+            vm((groups, zrows, width), BF16),
+            vm((groups, zrows * nz, width), BF16),
             dma((10,)),
             dma((3, 2)),
             dma((3, 2)),
@@ -699,47 +762,42 @@
             dma((2, CHUNKS, n - 1)),
             dma((2, CHUNKS, n - 1)),
             dma((2, CHUNKS, n - 1)),
-            dma((nz - 1,)),
-            dma((nz - 1,)),
-            dma((nz - 1,)),
-            dma((nz - 1,)),
-            dma((2, n - 1)),
-            dma((2, n - 1)),
-            dma((2, n - 1)),
-            dma((2, n - 1)),
-            dma((2, n)),
-            dma((2, n)),
+            dma((groups, nz - 1)),
+            dma((groups, nz - 1)),
+            dma((groups, nz - 1)),
+            dma((groups, nz - 1)),
+            dma((groups, 2, n - 1)),
+            dma((groups, 2, n - 1)),
+            dma((groups, 2, n - 1)),
+            dma((groups, 2, n - 1)),
+            dma((groups, 2, n)),
+            dma((groups, 2, n)),
         ],
         compiler_params=pltpu.CompilerParams(
-            collective_id=0, has_side_effects=True, vmem_limit_bytes=60 * 1024 * 1024
+            collective_id=0, has_side_effects=True, vmem_limit_bytes=40 * 1024 * 1024
         ),
     )(
-        prognostic.reshape(flat),
-        diffusivity.reshape(levels * LONS, 128),
-        mixing.reshape(2 * LONS, 128),
-        cotangent.reshape(flat),
-        tile_cols.reshape(tiles, 1, 128),
-        pad_mask.reshape(tiles, 1, 128),
-        tile_count,
-        w_in,
-        w_mid,
-        w_out,
+        *operands
     )
-    grad_mid, grad_out, grad_in = pl.pallas_call(
+    state, sgrad, grad_mid, grad_out, grad_in = pl.pallas_call(
         functools.partial(unscramble_kernel, half),
-        grid=(CHUNKS,),
         out_shape=(
+            jax.ShapeDtypeStruct(flat, F32),
+            jax.ShapeDtypeStruct(flat, F32),
             jax.ShapeDtypeStruct(w_mid.shape, F32),
             jax.ShapeDtypeStruct(w_out.shape, F32),
             jax.ShapeDtypeStruct(w_in.shape, F32),
         ),
-        in_specs=[pl.BlockSpec((2, 2, n, n, rows, width), lambda k: (0, 0, 0, 0, k, 0))],
-        out_specs=(
-            pl.BlockSpec((CHUNK_ROWS, units), lambda k: (jnp.minimum(k, CHUNKS - 2), 0)),
-            pl.BlockSpec(w_out.shape, lambda k: (0, 0)),
-            pl.BlockSpec(w_in.shape, lambda k: (0, 0)),
-        ),
-    )(full)
+        in_specs=[vmem_spec] * 3,
+        out_specs=(pl.BlockSpec(memory_space=pltpu.HBM),) * 5,
+        scratch_shapes=[
+            vm(w_mid.shape, F32),
+            vm(w_out.shape, F32),
+            vm(w_in.shape, F32),
+            dma((CHUNKS + 3,)),
+        ],
+        compiler_params=pltpu.CompilerParams(vmem_limit_bytes=16 * 1024 * 1024),
+    )(state, sgrad, full)
     return (
         state.reshape(prognostic.shape),
         sgrad.reshape(prognostic.shape),

time: 70.3 us -> 64.6 us (0.919)
  Pallas kernels: 67.3 us -> 63.3 us
  local copies, waits for them, and re-layouts: 1.41 us -> 0 us
    pallas_call x1, Pallas kernels: 5.65 us -> 2.58 us  [per_device(): pl.pallas_call(functools.partial(unscramble_kernel, half), out_shape=(jax...]
    unnamed x6 -> x0, local copies, waits for them, and re-layouts: 1.41 us -> none
    pallas_call x1, Pallas kernels: 61.7 us -> 60.7 us  [per_device(): pl.pallas_call(functools.partial(window_kernel, (n, nz, levels, fields //...]
where the time goes in v2:
time: 64.6 us; the launch traced here: 64.5 us
  Pallas kernels  63.3 us (98%)
  between operations  1.29 us (2%)
    pallas_call x1, Pallas kernels, per_device(): pl.pallas_call(functools.partial(window_kernel, (n, nz, levels, fields //...  60.7 us
    pallas_call x1, Pallas kernels, per_device(): pl.pallas_call(functools.partial(unscramble_kernel, half), out_shape=(jax...  2.58 us

profile of v2, /device:TPU:1, one launch (start us, length us, event | category | flops | bytes accessed | tf_op | source)
XLA Modules:
  0.0 64.5 jit_solution(4697572217448407235)
XLA Ops:
  1.3 60.7 %shard_map.137 = (f32[512,128]{1,0:T(8,128)S(1)}, f32[512,128]{1,0:T(8,128)S(1)}, bf16[2,2,4,4,160,128]{5,4,3,2,1,0:T(8,128)(2,1)S(1)}) custom-call(f32[512,128]{1,0:T(8,128)} %bitcast.8, f32[128,128]{1,0:T(8,128)} %bitcast.10, f32[8,128]{1,0:T(8,128)} %bitcast.11, f32[512,128]{1,0:T(8,128)} %bitcast.9, s32[3,1,128]{2,1,0:T(1,128)} %bitcast.12, ...), custom_call_target="tpu_custom_call" | custom-call | tf_op jit(solution)/shard_map/pallas_call | solution.py:704
  62.0 2.6 %shard_map.138 = (f32[512,128]{1,0:T(8,128)}, f32[512,128]{1,0:T(8,128)}, f32[1024,1024]{1,0:T(8,128)}, f32[128,1024]{1,0:T(8,128)}, f32[1024,128]{1,0:T(8,128)}) custom-call(f32[512,128]{1,0:T(8,128)S(1)} %get-tuple-element.13.state_ref, f32[512,128]{1,0:T(8,128)S(1)} %get-tuple-element.14.sgrad_ref, ...), custom_call_target="tpu_custom_call" | custom-call | tf_op jit(solution)/shard_map/pallas_call | solution.py:782
